TPU v7x, 512 devices: a whole 4x4x16 slice. The times are simulated.
512 devices in a mesh: scen: 32 (over y, x, core), space: 8 (over z_lo), tm: 2 (over z_hi).
Axes of the slice: x: 4, y: 4, z: 16 (z_hi: 2, z_lo: 8; z = z_hi * 8 + z_lo), core: 2. Of those that a mesh axis runs over, the one named last changes fastest.
Arguments:
- coupling: bfloat16 [32, 4, 8, 128, 512], P('scen', 'tm', 'space'), may hold values from -0.09375 to 0.09375
- leaf_rhs: float32 [32, 4, 8, 128], P('scen', 'tm', 'space'), may hold values from -6 to 6
- conductance: float32 [32, 4, 8, 128], P('scen', 'tm', 'space'), may hold values from 0.42 to 0.52
- compressor: int32 [32, 4, 8], P('scen', 'tm', 'space'), may hold values 0 or 1
- blocks: float32 [32, 4, 8, 128, 128], P('scen', 'tm', 'space'), may hold values from -2 to 8, as said below
- parent_of: int32 [32], P('scen'), may hold values from 0 to 7, as said below
- parent_mat: float32 [8, 512, 512], P(None, ('space', 'tm')), may hold values from -2 to 8, as said below
- parent_rhs: float32 [8, 512], P(None, ('space', 'tm')), may hold values from -6 to 6
- link: float32 [8, 512, 256], P(None, ('space', 'tm')), may hold values from -0.25 to 0.25
- root_mat: float32 [256, 256], replicated, may hold values from -2 to 8, as said below
- root_rhs: float32 [256], replicated, may hold values from -6 to 6
Outputs:
- leaf_move: float32 [32, 4, 8, 128], P('scen', 'tm', 'space')
- parent_at_leaf: float32 [32, 512], P('scen', ('space', 'tm'))
- root_step: float32 [256], replicated
Inputs may be any that keep to these rules, and one draw needn't show every extreme that they name: `parent_of`: leaves come in aligned runs of 4 in a row; all leaves of a run share one parent, and each parent owns exactly one run. `blocks`: each block is symmetric with eigenvalues of 1 or more. `parent_mat`: each matrix is symmetric with eigenvalues of 1 or more. `root_mat`: symmetric with eigenvalues of 1 or more.
All inputs are finite; a program needn't handle non-finite values. No bound on the sum of `compressor` on one device may be relied on, other than what follows from the above.
Results may differ from a plain program's by a relative error of at most 0.0003.
Values sent between devices are 32-bit elements; how exact they have to be, the bound alone decides.
No kernel may reach another device: no remote copies, remote signals or barrier semaphores. Data moves between devices by JAX's collectives and lax.ppermute only.
A program may use at most 64 MiB of HBM per device.

v0:
```python
import jax
import jax.numpy as jnp
from jax import lax
from jax.sharding import PartitionSpec as P

PARENTS = 8
ITERS = 6
HIGH = lax.Precision.HIGHEST


def extended(cells, sides, width):
    for axis, dim in sides:
        count = lax.axis_size(axis)
        ends = count - 1
        head = lax.slice_in_dim(cells, 0, width, axis=dim)
        tail = lax.slice_in_dim(cells, cells.shape[dim] - width, cells.shape[dim], axis=dim)
        cells = jnp.concatenate(
            [
                lax.ppermute(tail, axis, [(i, (i + 1) % count) for i in range(ends)]),
                cells,
                lax.ppermute(head, axis, [((i + 1) % count, i) for i in range(ends)]),
            ],
            axis=dim,
        )
    return cells


def from_partner(block, axis, bit):
    count = lax.axis_size(axis)
    route = []
    for low in range(count):
        high = low | 1 << bit
        if high != low and high < count:
            route += [(low, high), (high, low)]
    return lax.ppermute(block, axis, route)


def factor_solve(matrix, right):
    factor = lax.linalg.cholesky(matrix)
    forward = lax.linalg.triangular_solve(factor, right, left_side=True, lower=True)
    return lax.linalg.triangular_solve(
        factor, forward, left_side=True, lower=True, transpose_a=True
    )


def invert_blocks(matrices):
    identity = jnp.broadcast_to(jnp.eye(matrices.shape[-1], dtype=matrices.dtype), matrices.shape)
    return factor_solve(matrices, identity)


def beside_all(padded):
    return padded[2:, 1:-1] + padded[:-2, 1:-1] + padded[1:-1, 2:] + padded[1:-1, :-2]


def block_apply(inverse, field):
    if field.ndim == 4:
        return jnp.einsum("tsij,tsjc->tsic", inverse, field, precision=HIGH)
    return jnp.einsum("tsij,tsj->tsi", inverse, field, precision=HIGH)


def body(
    coupling,
    leaf_rhs,
    conductance,
    compressor,
    blocks,
    parent_of,
    parent_mat,
    parent_rhs,
    link,
    root_mat,
    root_rhs,
):
    dense = coupling[0].astype(jnp.float32)
    right = leaf_rhs[0]
    weight = conductance[0] * (1.0 + compressor[0].astype(jnp.float32)[..., None]) * 0.5
    column_weight = weight[..., None]
    own_blocks = blocks[0]
    inverse = invert_blocks(own_blocks)
    solved = block_apply(inverse, dense)
    pulled = block_apply(inverse, right)
    for sweep_index in range(ITERS - 1):
        outer, outer_vector = (
            extended(solved * column_weight, (("space", 1), ("tm", 0)), 1),
            extended(pulled * weight, (("space", 1), ("tm", 0)), 1),
        )
        solved = block_apply(inverse, dense + beside_all(outer) * column_weight)
        pulled = block_apply(inverse, right + beside_all(outer_vector) * weight)
    schur = jnp.einsum("tsic,tsid->cd", dense, solved, precision=HIGH)
    gather_term = jnp.einsum("tsic,tsi->c", dense, pulled, precision=HIGH)
    strip, gather_strip = (
        lax.psum_scatter(schur, ("space", "tm"), scatter_dimension=0, tiled=True),
        lax.psum_scatter(gather_term, ("space", "tm"), scatter_dimension=0, tiled=True),
    )
    parent_label = parent_of[0]
    parent_slots = (jnp.arange(PARENTS, dtype=jnp.int32) == parent_label).astype(jnp.float32)
    group = lax.axis_size("scen") // PARENTS
    for bit_index in range(group.bit_length() - 1):
        partner, partner_vector = from_partner((strip, gather_strip), "scen", bit_index)
        strip = strip + partner
        gather_strip = gather_strip + partner_vector
    hess_strip = jnp.einsum("p,pij->ij", parent_slots, parent_mat, precision=HIGH) + strip
    right_strip = gather_strip - jnp.einsum("p,pi->i", parent_slots, parent_rhs, precision=HIGH)
    link_strip = jnp.einsum("p,pin->in", parent_slots, link, precision=HIGH)
    hessian, reduced, own_link = (
        lax.all_gather(hess_strip, ("space", "tm"), axis=0, tiled=True),
        lax.all_gather(right_strip, ("space", "tm"), axis=0, tiled=True),
        lax.all_gather(link_strip, ("space", "tm"), axis=0, tiled=True),
    )
    link_solved = factor_solve(hessian, own_link)
    vector_solved = factor_solve(hessian, reduced[:, None])[:, 0]
    leader = (lax.axis_index("scen") % group == 0).astype(jnp.float32)
    root_term, right_term = lax.psum(
        (
            jnp.einsum("in,im->nm", own_link, link_solved, precision=HIGH) * leader,
            jnp.einsum("in,i->n", own_link, vector_solved, precision=HIGH) * leader,
        ),
        "scen",
    )
    root_step = factor_solve(root_mat + root_term, (root_rhs - right_term)[:, None])[:, 0]
    parent_step = vector_solved + jnp.einsum("in,n->i", link_solved, root_step, precision=HIGH)
    share_rows = parent_step.shape[0] // (lax.axis_size("space") * lax.axis_size("tm"))
    strip_index = lax.axis_index("space") * lax.axis_size("tm") + lax.axis_index("tm")
    parent_at_leaf = lax.dynamic_slice_in_dim(parent_step, strip_index * share_rows, share_rows)[
        None
    ]
    leaf_move = pulled - jnp.einsum("tsic,c->tsi", solved, parent_step, precision=HIGH)
    return (leaf_move[None], parent_at_leaf, root_step)


def solution(mesh):
    return jax.shard_map(
        body,
        mesh=mesh,
        in_specs=(
            P("scen", "tm", "space", None, None),
            P("scen", "tm", "space", None),
            P("scen", "tm", "space", None),
            P("scen", "tm", "space"),
            P("scen", "tm", "space", None, None),
            P("scen"),
            P(None, ("space", "tm"), None),
            P(None, ("space", "tm")),
            P(None, ("space", "tm"), None),
            P(),
            P(),
        ),
        out_specs=(P("scen", "tm", "space", None), P("scen", ("space", "tm")), P()),
        check_vma=False,
    )
```

profile of v0, /device:TPU:1, one launch (start us, length us, event | category | flops | bytes accessed | tf_op | source)
XLA Modules:
  0.0 1398.3 jit_solution(3951500692941909314)
XLA Ops:
  8.5 23.5 %custom-call.49 = f32[2,1,128,128]{3,2,1,0:T(8,128)S(1)} custom-call(f32[2,1,128,128]{3,2,1,0:T(8,128)S(1)} %fusion.111), custom_call_target="Cholesky" | custom-call | tf_op jit(solution)/shard_map/cholesky | solution.py:39
  32.2 19.7 %custom-call.50 = f32[2,1,1,128,128]{3,4,2,1,0:T(8,128)S(1)} custom-call(f32[2,1,1,128,128]{4,3,2,1,0:T(8,128)S(1)} %fusion.119), custom_call_target="InvertDiagBlocksLowerTriangular" | custom-call | tf_op jit(solution)/shard_map/triangular_solve | solution.py:41
  59.1 6.4 collective-permute-done.20
  70.1 17.1 %collective-permute-start.23 = (f32[1,3,128,512]{3,2,0,1:T(8,128)S(1)}, f32[1,3,128,512]{3,2,0,1:T(8,128)S(1)}, u32[]{:S(2)}, u32[]{:S(2)}) collective-permute-start(f32[1,3,128,512]{3,2,0,1:T(8,128)S(1)} %get-tuple-element.52), channel_id=1, source_target_pairs={{0,1},{2,3},{4,5},{6,7},{8,9},{10,11},{12,13},{14,15},{16,17},{18,... | collective-permute-start | bytes 2359304 | tf_op jit(solution)/shard_map/ppermute | solution.py:19
  88.5 17.9 %collective-permute-done.23 = f32[1,3,128,512]{3,2,0,1:T(8,128)S(1)} collective-permute-done((f32[1,3,128,512]{3,2,0,1:T(8,128)S(1)}, f32[1,3,128,512]{3,2,0,1:T(8,128)S(1)}, u32[]{:S(2)}, u32[]{:S(2)}) %collective-permute-start.23) | collective-permute-done | bytes 786464 | tf_op jit(solution)/shard_map/ppermute | solution.py:19
  106.4 17.5 %collective-permute-done.22 = f32[1,3,128,512]{3,2,0,1:T(8,128)S(1)} collective-permute-done((f32[1,3,128,512]{3,2,0,1:T(8,128)S(1)}, f32[1,3,128,512]{3,2,0,1:T(8,128)S(1)}, u32[]{:S(2)}, u32[]{:S(2)}) %collective-permute-start.22) | collective-permute-done | bytes 786464 | tf_op jit(solution)/shard_map/ppermute | solution.py:21
  124.6 43.4 %collective-permute-start.24 = (f32[2,1,128,512]{3,2,0,1:T(8,128)S(1)}, f32[2,1,128,512]{3,2,0,1:T(8,128)S(1)}, u32[]{:S(2)}, u32[]{:S(2)}) collective-permute-start(f32[2,1,128,512]{3,2,0,1:T(8,128)S(1)} %fusion.4), channel_id=1, source_target_pairs={{0,2},{2,4},{4,6},{6,8},{8,10},{10,12},{12,14},{1,3},{3,5},{5,7},{... | collective-permute-start | bytes 1572872 | tf_op jit(solution)/shard_map/ppermute | solution.py:19
  169.3 8.1 collective-permute-done.24
  184.9 7.6 collective-permute-done.27
  192.4 61.9 %collective-permute-done.26 = f32[1,3,128,512]{3,2,0,1:T(8,128)S(1)} collective-permute-done((f32[1,3,128,512]{3,2,0,1:T(8,128)S(1)}, f32[1,3,128,512]{3,2,0,1:T(8,128)S(1)}, u32[]{:S(2)}, u32[]{:S(2)}) %collective-permute-start.26) | collective-permute-done | bytes 786464 | tf_op jit(solution)/shard_map/ppermute | solution.py:21
  255.1 8.0 collective-permute-start.28
  264.3 8.7 collective-permute-done.28
  280.1 11.7 collective-permute-done.31
  291.8 14.2 %collective-permute-done.30 = f32[1,3,128,512]{3,2,0,1:T(8,128)S(1)} collective-permute-done((f32[1,3,128,512]{3,2,0,1:T(8,128)S(1)}, f32[1,3,128,512]{3,2,0,1:T(8,128)S(1)}, u32[]{:S(2)}, u32[]{:S(2)}) %collective-permute-start.30) | collective-permute-done | bytes 786464 | tf_op jit(solution)/shard_map/ppermute | solution.py:21
  306.8 53.8 %collective-permute-start.32 = (f32[2,1,128,512]{3,2,0,1:T(8,128)S(1)}, f32[2,1,128,512]{3,2,0,1:T(8,128)S(1)}, u32[]{:S(2)}, u32[]{:S(2)}) collective-permute-start(f32[2,1,128,512]{3,2,0,1:T(8,128)S(1)} %fusion.2), channel_id=1, source_target_pairs={{0,2},{2,4},{4,6},{6,8},{8,10},{10,12},{12,14},{1,3},{3,5},{5,7},{... | collective-permute-start | bytes 1572872 | tf_op jit(solution)/shard_map/ppermute | solution.py:19
  361.9 9.3 collective-permute-done.32
  382.7 18.1 %collective-permute-done = f32[2,1,128]{2,0,1:T(2,128)S(1)} collective-permute-done((f32[2,1,128]{2,0,1:T(2,128)S(1)}, f32[2,1,128]{2,0,1:T(2,128)S(1)}, u32[]{:S(2)}, u32[]{:S(2)}) %collective-permute-start) | collective-permute-done | bytes 1056 | tf_op jit(solution)/shard_map/ppermute | solution.py:19
  400.8 44.3 %collective-permute-done.1 = f32[2,1,128]{2,0,1:T(2,128)S(1)} collective-permute-done((f32[2,1,128]{2,0,1:T(2,128)S(1)}, f32[2,1,128]{2,0,1:T(2,128)S(1)}, u32[]{:S(2)}, u32[]{:S(2)}) %collective-permute-start.1) | collective-permute-done | bytes 1056 | tf_op jit(solution)/shard_map/ppermute | solution.py:21
  445.1 11.7 collective-permute-start.3
  462.2 7.8 collective-permute-done.2
  474.4 12.5 collective-permute-start.39
  491.7 129.8 %all_gather.11 = f32[512,256]{1,0:T(8,128)S(1)} all-gather(f32[32,256]{1,0:T(8,128)S(1)} %bitcast.421), channel_id=1, replica_groups=mesh['scen'=32,'space'=8,'tm'=2] {'space','tm'}, dimensions={0}, use_global_device_ids=true | all-gather | bytes 557056 | tf_op jit(solution)/shard_map/all_gather | solution.py:108
  632.5 7.6 collective-permute-done.6
  640.5 6.8 collective-permute-start.8
  658.2 11.7 collective-permute-done.10
  670.3 10.3 collective-permute-start.12
  682.1 133.1 %reduce-scatter.4.cloned.1.call-done = f32[32,512]{1,0:T(8,128)} async-done(((f32[512,512]{1,0:T(8,128)}), f32[32,512]{1,0:T(8,128)}) %reduce-scatter.4.cloned.1.call-update) | async-done | bytes 65552
  816.2 18.8 %collective-permute-start.40 = (f32[32,512]{0,1:T(8,128)S(1)}, f32[32,512]{0,1:T(8,128)S(1)}, u32[]{:S(2)}, u32[]{:S(2)}) collective-permute-start(f32[32,512]{0,1:T(8,128)S(1)} %copy.80), channel_id=1, source_target_pairs={{0,16},{16,0},{32,48},{48,32},{64,80},{80,64},{96,112},{112,96},{1... | collective-permute-start | bytes 196616 | tf_op jit(solution)/shard_map/ppermute | solution.py:35
  846.4 6.6 collective-permute-done.14
  865.2 9.6 collective-permute-done.18
  875.5 61.5 %all-reduce.3 = f32[512]{0:T(512)S(1)} all-reduce(f32[512]{0:T(512)S(1)} %bitcast.439), channel_id=3, replica_groups=mesh['scen'=32,'space'=8,'tm'=2] {'space','tm'}, use_global_device_ids=true, to_apply=%region_11.14.clone | all-reduce | flops 512 | bytes 4096
  937.0 18.8 %collective-permute-start.42 = (f32[32]{0:T(128)S(1)}, f32[32]{0:T(128)S(1)}, u32[]{:S(2)}, u32[]{:S(2)}) collective-permute-start(f32[32]{0:T(128)S(1)} %dynamic-slice.8), channel_id=1, source_target_pairs={{0,16},{16,0},{32,48},{48,32},{64,80},{80,64},{96,112},{112,96},{1... | collective-permute-start | bytes 392 | tf_op jit(solution)/shard_map/ppermute | solution.py:35
  961.1 65.8 %all-reduce.2 = f32[512]{0:T(512)S(1)} all-reduce(f32[512]{0:T(512)S(1)} %subtract_dynamic-update-slice_fusion), channel_id=1, replica_groups=mesh['scen'=32,'space'=8,'tm'=2] {'space','tm'}, use_global_device_ids=true, to_apply=%add.2 | all-reduce | flops 512 | bytes 4096
  1029.9 11.7 custom-call.55
  1041.8 9.8 custom-call.56
  1054.5 11.7 custom-call.57
  1066.2 10.0 custom-call.58
  1077.8 11.7 custom-call.59
  1089.5 9.8 custom-call.60
  1100.8 11.9 custom-call.61
  1117.3 10.4 while.2
  1127.7 40.1 %custom-call.51 = f32[4,128,128]{1,2,0:T(8,128)S(1)} custom-call(f32[4,128,128]{2,1,0:T(8,128)} %get-tuple-element.12), custom_call_target="InvertDiagBlocksLowerTriangular" | custom-call | tf_op jit(solution)/shard_map/triangular_solve | solution.py:41
  1177.4 75.5 %psum.15 = f32[256]{0:T(256)S(1)} all-reduce(f32[256]{0:T(256)S(1)} %broadcast_multiply_fusion), channel_id=1, replica_groups=mesh['scen'=32,'space'=8,'tm'=2] {'scen'}, use_global_device_ids=true, to_apply=%region_17.20 | all-reduce | flops 256 | bytes 2048 | tf_op jit(solution)/shard_map/psum | solution.py:113
  1252.9 70.8 %all-reduce.6.cloned.1.call-done = f32[256,256]{0,1:T(8,128)} async-done(((f32[256,256]{0,1:T(8,128)}), f32[256,256]{0,1:T(8,128)}) %all-reduce.6.cloned.1.call-update) | async-done | bytes 262160 | tf_op jit(solution)/shard_map/psum | solution.py:113
  1324.9 11.7 cholesky.104
  1336.6 9.8 custom-call.62
  1346.9 11.7 cholesky.114
  1366.6 20.8 %custom-call.52 = f32[2,128,128]{1,2,0:T(8,128)S(1)} custom-call(f32[2,128,128]{2,1,0:T(8,128)} %get-tuple-element.20), custom_call_target="InvertDiagBlocksLowerTriangular" | custom-call | tf_op jit(solution)/shard_map/triangular_solve | solution.py:41
  (274 shorter events, 161.7 us)
Async XLA Ops:
  7.2 624.6 %copy-start = (f32[8,32,512]{2,1,0:T(8,128)S(1)}, f32[8,32,512]{2,1,0:T(8,128)}, u32[]{:S(2)}) copy-start(f32[8,32,512]{2,1,0:T(8,128)} %param.20) | copy-start | bytes 1572868
  7.2 808.0 %reduce-scatter.4.cloned.1.call-start = ((), (), s32[]{:S(2)}) async-start(), calls=%async_computation.3 | async-start | bytes 1114112
  53.4 12.1 collective-permute-start.20
  57.8 11.9 collective-permute-start.21
  70.1 36.3 %collective-permute-start.23 = (f32[1,3,128,512]{3,2,0,1:T(8,128)S(1)}, f32[1,3,128,512]{3,2,0,1:T(8,128)S(1)}, u32[]{:S(2)}, u32[]{:S(2)}) collective-permute-start(f32[1,3,128,512]{3,2,0,1:T(8,128)S(1)} %get-tuple-element.52), channel_id=1, source_target_pairs={{0,1},{2,3},{4,5},{6,7},{8,9},{10,11},{12,13},{14,15},{16,17},{18,... | collective-permute-start | bytes 2359304 | tf_op jit(solution)/shard_map/ppermute | solution.py:19
  87.2 36.7 %collective-permute-start.22 = (f32[1,3,128,512]{3,2,0,1:T(8,128)S(1)}, f32[1,3,128,512]{3,2,0,1:T(8,128)S(1)}, u32[]{:S(2)}, u32[]{:S(2)}) collective-permute-start(f32[1,3,128,512]{3,2,0,1:T(8,128)S(1)} %get-tuple-element.51), channel_id=1, source_target_pairs={{1,0},{3,2},{5,4},{7,6},{9,8},{11,10},{13,12},{15,14},{17,16},{19,... | collective-permute-start | bytes 2359304 | tf_op jit(solution)/shard_map/ppermute | solution.py:21
  124.6 52.9 %collective-permute-start.24 = (f32[2,1,128,512]{3,2,0,1:T(8,128)S(1)}, f32[2,1,128,512]{3,2,0,1:T(8,128)S(1)}, u32[]{:S(2)}, u32[]{:S(2)}) collective-permute-start(f32[2,1,128,512]{3,2,0,1:T(8,128)S(1)} %fusion.4), channel_id=1, source_target_pairs={{0,2},{2,4},{4,6},{6,8},{8,10},{10,12},{12,14},{1,3},{3,5},{5,7},{... | collective-permute-start | bytes 1572872 | tf_op jit(solution)/shard_map/ppermute | solution.py:19
  168.0 13.3 collective-permute-start.25
  181.7 10.7 collective-permute-start.27
  183.6 70.8 %collective-permute-start.26 = (f32[1,3,128,512]{3,2,0,1:T(8,128)S(1)}, f32[1,3,128,512]{3,2,0,1:T(8,128)S(1)}, u32[]{:S(2)}, u32[]{:S(2)}) collective-permute-start(f32[1,3,128,512]{3,2,0,1:T(8,128)S(1)} %get-tuple-element.49), channel_id=1, source_target_pairs={{1,0},{3,2},{5,4},{7,6},{9,8},{11,10},{13,12},{15,14},{17,16},{19,... | collective-permute-start | bytes 2359304 | tf_op jit(solution)/shard_map/ppermute | solution.py:21
  255.1 17.9 %collective-permute-start.28 = (f32[2,1,128,512]{3,2,0,1:T(8,128)S(1)}, f32[2,1,128,512]{3,2,0,1:T(8,128)S(1)}, u32[]{:S(2)}, u32[]{:S(2)}) collective-permute-start(f32[2,1,128,512]{3,2,0,1:T(8,128)S(1)} %fusion.3), channel_id=1, source_target_pairs={{0,2},{2,4},{4,6},{6,8},{8,10},{10,12},{12,14},{1,3},{3,5},{5,7},{... | collective-permute-start | bytes 1572872 | tf_op jit(solution)/shard_map/ppermute | solution.py:19
  263.0 13.8 collective-permute-start.29
  277.3 14.5 %collective-permute-start.31 = (f32[1,3,128,512]{3,2,0,1:T(8,128)S(1)}, f32[1,3,128,512]{3,2,0,1:T(8,128)S(1)}, u32[]{:S(2)}, u32[]{:S(2)}) collective-permute-start(f32[1,3,128,512]{3,2,0,1:T(8,128)S(1)} %get-tuple-element.48), channel_id=1, source_target_pairs={{0,1},{2,3},{4,5},{6,7},{8,9},{10,11},{12,13},{14,15},{16,17},{18,... | collective-permute-start | bytes 2359304 | tf_op jit(solution)/shard_map/ppermute | solution.py:19
  278.6 27.4 %collective-permute-start.30 = (f32[1,3,128,512]{3,2,0,1:T(8,128)S(1)}, f32[1,3,128,512]{3,2,0,1:T(8,128)S(1)}, u32[]{:S(2)}, u32[]{:S(2)}) collective-permute-start(f32[1,3,128,512]{3,2,0,1:T(8,128)S(1)} %get-tuple-element.47), channel_id=1, source_target_pairs={{1,0},{3,2},{5,4},{7,6},{9,8},{11,10},{13,12},{15,14},{17,16},{19,... | collective-permute-start | bytes 2359304 | tf_op jit(solution)/shard_map/ppermute | solution.py:21
  306.8 64.4 %collective-permute-start.32 = (f32[2,1,128,512]{3,2,0,1:T(8,128)S(1)}, f32[2,1,128,512]{3,2,0,1:T(8,128)S(1)}, u32[]{:S(2)}, u32[]{:S(2)}) collective-permute-start(f32[2,1,128,512]{3,2,0,1:T(8,128)S(1)} %fusion.2), channel_id=1, source_target_pairs={{0,2},{2,4},{4,6},{6,8},{8,10},{10,12},{12,14},{1,3},{3,5},{5,7},{... | collective-permute-start | bytes 1572872 | tf_op jit(solution)/shard_map/ppermute | solution.py:19
  360.6 14.4 %collective-permute-start.33 = (f32[2,1,128,512]{3,2,0,1:T(8,128)S(1)}, f32[2,1,128,512]{3,2,0,1:T(8,128)S(1)}, u32[]{:S(2)}, u32[]{:S(2)}) collective-permute-start(f32[2,1,128,512]{3,2,0,1:T(8,128)S(1)} %fusion.2), channel_id=1, source_target_pairs={{2,0},{4,2},{6,4},{8,6},{10,8},{12,10},{14,12},{3,1},{5,3},{7,5},{... | collective-permute-start | bytes 1572872 | tf_op jit(solution)/shard_map/ppermute | solution.py:21
  375.4 82.8 %collective-permute-start.35 = (f32[1,3,128,512]{3,2,0,1:T(8,128)S(1)}, f32[1,3,128,512]{3,2,0,1:T(8,128)S(1)}, u32[]{:S(2)}, u32[]{:S(2)}) collective-permute-start(f32[1,3,128,512]{3,2,0,1:T(8,128)S(1)} %get-tuple-element.46), channel_id=1, source_target_pairs={{0,1},{2,3},{4,5},{6,7},{8,9},{10,11},{12,13},{14,15},{16,17},{18,... | collective-permute-start | bytes 2359304 | tf_op jit(solution)/shard_map/ppermute | solution.py:19
  377.3 81.0 %collective-permute-start.34 = (f32[1,3,128,512]{3,2,0,1:T(8,128)S(1)}, f32[1,3,128,512]{3,2,0,1:T(8,128)S(1)}, u32[]{:S(2)}, u32[]{:S(2)}) collective-permute-start(f32[1,3,128,512]{3,2,0,1:T(8,128)S(1)} %get-tuple-element.45), channel_id=1, source_target_pairs={{1,0},{3,2},{5,4},{7,6},{9,8},{11,10},{13,12},{15,14},{17,16},{19,... | collective-permute-start | bytes 2359304 | tf_op jit(solution)/shard_map/ppermute | solution.py:21
  378.6 22.2 %collective-permute-start = (f32[2,1,128]{2,0,1:T(2,128)S(1)}, f32[2,1,128]{2,0,1:T(2,128)S(1)}, u32[]{:S(2)}, u32[]{:S(2)}) collective-permute-start(f32[2,1,128]{2,0,1:T(2,128)S(1)} %get-tuple-element.37), channel_id=1, source_target_pairs={{0,2},{2,4},{4,6},{6,8},{8,10},{10,12},{12,14},{1,3},{3,5},{5,7},{... | collective-permute-start | bytes 3080 | tf_op jit(solution)/shard_map/ppermute | solution.py:19
  380.8 64.3 %collective-permute-start.1 = (f32[2,1,128]{2,0,1:T(2,128)S(1)}, f32[2,1,128]{2,0,1:T(2,128)S(1)}, u32[]{:S(2)}, u32[]{:S(2)}) collective-permute-start(f32[2,1,128]{2,0,1:T(2,128)S(1)} %get-tuple-element.37), channel_id=1, source_target_pairs={{2,0},{4,2},{6,4},{8,6},{10,8},{12,10},{14,12},{3,1},{5,3},{7,5},{... | collective-permute-start | bytes 3080 | tf_op jit(solution)/shard_map/ppermute | solution.py:21
  445.1 17.1 %collective-permute-start.3 = (f32[1,3,128]{2,0,1:T(1,128)S(1)}, f32[1,3,128]{2,0,1:T(1,128)S(1)}, u32[]{:S(2)}, u32[]{:S(2)}) collective-permute-start(f32[1,3,128]{2,0,1:T(1,128)S(1)} %get-tuple-element.76), channel_id=1, source_target_pairs={{0,1},{2,3},{4,5},{6,7},{8,9},{10,11},{12,13},{14,15},{16,17},{18,... | collective-permute-start | bytes 4616 | tf_op jit(solution)/shard_map/ppermute | solution.py:19
  456.8 13.2 collective-permute-start.2
  459.0 11.4 collective-permute-start.36
  460.5 13.5 collective-permute-start.37
  474.4 153.9 %collective-permute-start.39 = (f32[1,3,128,512]{3,2,0,1:T(8,128)S(1)}, f32[1,3,128,512]{3,2,0,1:T(8,128)S(1)}, u32[]{:S(2)}, u32[]{:S(2)}) collective-permute-start(f32[1,3,128,512]{3,2,0,1:T(8,128)S(1)} %get-tuple-element.44), channel_id=1, source_target_pairs={{0,1},{2,3},{4,5},{6,7},{8,9},{10,11},{12,13},{14,15},{16,17},{18,... | collective-permute-start | bytes 2359304 | tf_op jit(solution)/shard_map/ppermute | solution.py:19
  486.9 141.4 %collective-permute-start.38 = (f32[1,3,128,512]{3,2,0,1:T(8,128)S(1)}, f32[1,3,128,512]{3,2,0,1:T(8,128)S(1)}, u32[]{:S(2)}, u32[]{:S(2)}) collective-permute-start(f32[1,3,128,512]{3,2,0,1:T(8,128)S(1)} %get-tuple-element.43), channel_id=1, source_target_pairs={{1,0},{3,2},{5,4},{7,6},{9,8},{11,10},{13,12},{15,14},{17,16},{19,... | collective-permute-start | bytes 2359304 | tf_op jit(solution)/shard_map/ppermute | solution.py:21
  488.2 133.3 %collective-permute-start.4 = (f32[2,1,128]{2,0,1:T(2,128)S(1)}, f32[2,1,128]{2,0,1:T(2,128)S(1)}, u32[]{:S(2)}, u32[]{:S(2)}) collective-permute-start(f32[2,1,128]{2,0,1:T(2,128)S(1)} %multiply_bitcast_fusion.3), channel_id=1, source_target_pairs={{0,2},{2,4},{4,6},{6,8},{8,10},{10,12},{12,14},{1,3},{3,5},{5,7},{... | collective-permute-start | bytes 3080 | tf_op jit(solution)/shard_map/ppermute | solution.py:19
  490.4 131.1 %collective-permute-start.5 = (f32[2,1,128]{2,0,1:T(2,128)S(1)}, f32[2,1,128]{2,0,1:T(2,128)S(1)}, u32[]{:S(2)}, u32[]{:S(2)}) collective-permute-start(f32[2,1,128]{2,0,1:T(2,128)S(1)} %multiply_bitcast_fusion.3), channel_id=1, source_target_pairs={{2,0},{4,2},{6,4},{8,6},{10,8},{12,10},{14,12},{3,1},{5,3},{7,5},{... | collective-permute-start | bytes 3080 | tf_op jit(solution)/shard_map/ppermute | solution.py:21
  621.5 11.0 collective-permute-start.7
  626.9 13.2 collective-permute-start.6
  631.8 395.2 %all-gather.2.cloned.1.call-start = ((), (), s32[]{:S(2)}) async-start(), calls=%async_computation.1 | async-start | bytes 1114112 | tf_op jit(solution)/shard_map/all_gather | solution.py:106
  640.5 8.3 collective-permute-start.8
  647.3 4.6 collective-permute-start.9
  652.0 6.2 collective-permute-start.11
  656.9 13.0 collective-permute-start.10
  670.3 164.7 %collective-permute-start.12 = (f32[2,1,128]{2,0,1:T(2,128)S(1)}, f32[2,1,128]{2,0,1:T(2,128)S(1)}, u32[]{:S(2)}, u32[]{:S(2)}) collective-permute-start(f32[2,1,128]{2,0,1:T(2,128)S(1)} %multiply_bitcast_fusion.1), channel_id=1, source_target_pairs={{0,2},{2,4},{4,6},{6,8},{8,10},{10,12},{12,14},{1,3},{3,5},{5,7},{... | collective-permute-start | bytes 3080 | tf_op jit(solution)/shard_map/ppermute | solution.py:19
  680.6 154.4 %collective-permute-start.13 = (f32[2,1,128]{2,0,1:T(2,128)S(1)}, f32[2,1,128]{2,0,1:T(2,128)S(1)}, u32[]{:S(2)}, u32[]{:S(2)}) collective-permute-start(f32[2,1,128]{2,0,1:T(2,128)S(1)} %multiply_bitcast_fusion.1), channel_id=1, source_target_pairs={{2,0},{4,2},{6,4},{8,6},{10,8},{12,10},{14,12},{3,1},{5,3},{7,5},{... | collective-permute-start | bytes 3080 | tf_op jit(solution)/shard_map/ppermute | solution.py:21
  816.2 19.9 %collective-permute-start.40 = (f32[32,512]{0,1:T(8,128)S(1)}, f32[32,512]{0,1:T(8,128)S(1)}, u32[]{:S(2)}, u32[]{:S(2)}) collective-permute-start(f32[32,512]{0,1:T(8,128)S(1)} %copy.80), channel_id=1, source_target_pairs={{0,16},{16,0},{32,48},{48,32},{64,80},{80,64},{96,112},{112,96},{1... | collective-permute-start | bytes 196616 | tf_op jit(solution)/shard_map/ppermute | solution.py:35
  836.2 9.4 collective-permute-start.41
  838.1 8.3 collective-permute-start.15
  840.0 13.0 collective-permute-start.14
  846.4 477.3 %all-reduce.6.cloned.1.call-start = ((), (), s32[]{:S(2)}) async-start(), calls=%async_computation.2 | async-start | bytes 524288 | tf_op jit(solution)/shard_map/psum | solution.py:113
  853.4 3.6 collective-permute-start.16
  855.6 4.3 collective-permute-start.17
  860.0 5.3 collective-permute-start.19
  861.8 13.0 collective-permute-start.18
  937.0 19.6 %collective-permute-start.42 = (f32[32]{0:T(128)S(1)}, f32[32]{0:T(128)S(1)}, u32[]{:S(2)}, u32[]{:S(2)}) collective-permute-start(f32[32]{0:T(128)S(1)} %dynamic-slice.8), channel_id=1, source_target_pairs={{0,16},{16,0},{32,48},{48,32},{64,80},{80,64},{96,112},{112,96},{1... | collective-permute-start | bytes 392 | tf_op jit(solution)/shard_map/ppermute | solution.py:35
  956.7 4.3 collective-permute-start.43
  (14 other events, 720.0 us)
Sparse Core Ops, SparseCore 0:
  631.9 183.3 reduce-scatter.3
  846.5 164.8 all-gather.1
  1177.2 146.4 all-reduce.5
where the time goes:
time: 1410 us; the launch traced here: 1400 us
  waiting for transfers between devices  506 us (36%)
  blocking collectives  333 us (24%)
  starting transfers between devices  263 us (19%)
  other arithmetic  222 us (16%)
  local copies, waits for them, and re-layouts  27 us (2%)
  matrix products  26.3 us (2%)
  between operations  21.4 us (2%)
    ppermute x20, waiting for transfers between devices, extended(): lax.ppermute(head, axis, [((i + 1) % count, i) for i in range(ends)])  207 us
    ppermute x20, starting transfers between devices, extended(): lax.ppermute(tail, axis, [(i, (i + 1) % count) for i in range(ends)])  195 us
    another operation x25, other arithmetic, factor_solve(): factor = lax.linalg.cholesky(matrix)  137 us
    unnamed x4, waiting for transfers between devices  133 us
    all_gather x1, blocking collectives, body(): lax.all_gather(link_strip, ('space', 'tm'), axis=0, tiled=True)  130 us
    unnamed x2, blocking collectives  127 us
    ppermute x20, waiting for transfers between devices, extended(): lax.ppermute(tail, axis, [(i, (i + 1) % count) for i in range(ends)])  87.8 us
    another operation x11, other arithmetic, factor_solve(): lax.linalg.triangular_solve(factor, forward, left_side=True, lower=True,...  81.4 us
  transfers between devices with their start and end apart: 47, of which 30 were waited for; matrix products, arithmetic and copies ran while one was open for 1% of the time, Pallas kernels for 0%

commit v1 on v0

--- a/solution.py
+++ b/solution.py
@@ -105,7 +105,12 @@
     hessian, reduced, own_link = (
         lax.all_gather(hess_strip, ("space", "tm"), axis=0, tiled=True),
         lax.all_gather(right_strip, ("space", "tm"), axis=0, tiled=True),
-        lax.all_gather(link_strip, ("space", "tm"), axis=0, tiled=True),
+        jnp.concatenate(
+            lax.all_to_all(
+                jnp.stack([link_strip] * lax.axis_size(("space", "tm"))), ("space", "tm"), 0, 0
+            ),
+            axis=0,
+        ),
     )
     link_solved = factor_solve(hessian, own_link)
     vector_solved = factor_solve(hessian, reduced[:, None])[:, 0]

time: 1410 us -> 1330 us (0.943)
  blocking collectives: 333 us -> 207 us
  starting transfers between devices: 263 us -> 315 us
    all_gather x1 -> x0, blocking collectives: 130 us -> none  [body(): lax.all_gather(link_strip, ('space', 'tm'), axis=0, tiled=True)]
    ppermute x20, starting transfers between devices: 195 us -> 233 us  [extended(): lax.ppermute(tail, axis, [(i, (i + 1) % count) for i in range(ends)])]
  transfers between devices with their start and end apart: 47 -> 48, of which waited for: 30 -> 30; matrix products, arithmetic and copies ran while one was open for 1% -> 1% of each run, Pallas kernels for 0% -> 0%
where the time goes in v1:
time: 1330 us; the launch traced here: 1320 us
  waiting for transfers between devices  497 us (37%)
  starting transfers between devices  315 us (24%)
  other arithmetic  222 us (17%)
  blocking collectives  207 us (16%)
  local copies, waits for them, and re-layouts  29.8 us (2%)
  matrix products  27.3 us (2%)
  between operations  21.3 us (2%)
    ppermute x20, starting transfers between devices, extended(): lax.ppermute(tail, axis, [(i, (i + 1) % count) for i in range(ends)])  233 us
    ppermute x20, waiting for transfers between devices, extended(): lax.ppermute(head, axis, [((i + 1) % count, i) for i in range(ends)])  204 us
    another operation x25, other arithmetic, factor_solve(): factor = lax.linalg.cholesky(matrix)  137 us
    unnamed x2, blocking collectives  132 us
    unnamed x4, waiting for transfers between devices  121 us
    ppermute x20, waiting for transfers between devices, extended(): lax.ppermute(tail, axis, [(i, (i + 1) % count) for i in range(ends)])  88.4 us
    another operation x11, other arithmetic, factor_solve(): lax.linalg.triangular_solve(factor, forward, left_side=True, lower=True,...  81.4 us
    psum x1, blocking collectives, body(): lax.psum((jnp.einsum('in,im->nm', own_link, link_solved, precision=HIGH)...  75.3 us
  transfers between devices with their start and end apart: 48, of which 30 were waited for; matrix products, arithmetic and copies ran while one was open for 1% of the time, Pallas kernels for 0%

profile of v1, /device:TPU:1, one launch (start us, length us, event | category | flops | bytes accessed | tf_op | source)
XLA Modules:
  0.0 1319.3 jit_solution(17564980259713709307)
XLA Ops:
  8.5 23.5 %custom-call.49 = f32[2,1,128,128]{3,2,1,0:T(8,128)S(1)} custom-call(f32[2,1,128,128]{3,2,1,0:T(8,128)S(1)} %fusion.109), custom_call_target="Cholesky" | custom-call | tf_op jit(solution)/shard_map/cholesky | solution.py:39
  32.2 19.7 %custom-call.50 = f32[2,1,1,128,128]{3,4,2,1,0:T(8,128)S(1)} custom-call(f32[2,1,1,128,128]{4,3,2,1,0:T(8,128)S(1)} %fusion.117), custom_call_target="InvertDiagBlocksLowerTriangular" | custom-call | tf_op jit(solution)/shard_map/triangular_solve | solution.py:41
  70.1 17.1 %collective-permute-start.23 = (f32[1,3,128,512]{3,2,0,1:T(8,128)S(1)}, f32[1,3,128,512]{3,2,0,1:T(8,128)S(1)}, u32[]{:S(2)}, u32[]{:S(2)}) collective-permute-start(f32[1,3,128,512]{3,2,0,1:T(8,128)S(1)} %get-tuple-element.52), channel_id=1, source_target_pairs={{0,1},{2,3},{4,5},{6,7},{8,9},{10,11},{12,13},{14,15},{16,17},{18,... | collective-permute-start | bytes 2359304 | tf_op jit(solution)/shard_map/ppermute | solution.py:19
  88.5 17.9 %collective-permute-done.23 = f32[1,3,128,512]{3,2,0,1:T(8,128)S(1)} collective-permute-done((f32[1,3,128,512]{3,2,0,1:T(8,128)S(1)}, f32[1,3,128,512]{3,2,0,1:T(8,128)S(1)}, u32[]{:S(2)}, u32[]{:S(2)}) %collective-permute-start.23) | collective-permute-done | bytes 786464 | tf_op jit(solution)/shard_map/ppermute | solution.py:19
  106.4 17.5 %collective-permute-done.22 = f32[1,3,128,512]{3,2,0,1:T(8,128)S(1)} collective-permute-done((f32[1,3,128,512]{3,2,0,1:T(8,128)S(1)}, f32[1,3,128,512]{3,2,0,1:T(8,128)S(1)}, u32[]{:S(2)}, u32[]{:S(2)}) %collective-permute-start.22) | collective-permute-done | bytes 786464 | tf_op jit(solution)/shard_map/ppermute | solution.py:21
  124.6 43.4 %collective-permute-start.24 = (f32[2,1,128,512]{3,2,0,1:T(8,128)S(1)}, f32[2,1,128,512]{3,2,0,1:T(8,128)S(1)}, u32[]{:S(2)}, u32[]{:S(2)}) collective-permute-start(f32[2,1,128,512]{3,2,0,1:T(8,128)S(1)} %fusion.4), channel_id=1, source_target_pairs={{0,2},{2,4},{4,6},{6,8},{8,10},{10,12},{12,14},{1,3},{3,5},{5,7},{... | collective-permute-start | bytes 1572872 | tf_op jit(solution)/shard_map/ppermute | solution.py:19
  169.3 8.1 collective-permute-done.24
  184.8 7.6 collective-permute-done.27
  192.4 61.9 %collective-permute-done.26 = f32[1,3,128,512]{3,2,0,1:T(8,128)S(1)} collective-permute-done((f32[1,3,128,512]{3,2,0,1:T(8,128)S(1)}, f32[1,3,128,512]{3,2,0,1:T(8,128)S(1)}, u32[]{:S(2)}, u32[]{:S(2)}) %collective-permute-start.26) | collective-permute-done | bytes 786464 | tf_op jit(solution)/shard_map/ppermute | solution.py:21
  255.0 8.1 collective-permute-start.28
  264.4 8.7 collective-permute-done.28
  280.3 12.2 collective-permute-done.31
  292.5 14.1 %collective-permute-done.30 = f32[1,3,128,512]{3,2,0,1:T(8,128)S(1)} collective-permute-done((f32[1,3,128,512]{3,2,0,1:T(8,128)S(1)}, f32[1,3,128,512]{3,2,0,1:T(8,128)S(1)}, u32[]{:S(2)}, u32[]{:S(2)}) %collective-permute-start.30) | collective-permute-done | bytes 786464 | tf_op jit(solution)/shard_map/ppermute | solution.py:21
  307.3 53.3 %collective-permute-start.32 = (f32[2,1,128,512]{3,2,0,1:T(8,128)S(1)}, f32[2,1,128,512]{3,2,0,1:T(8,128)S(1)}, u32[]{:S(2)}, u32[]{:S(2)}) collective-permute-start(f32[2,1,128,512]{3,2,0,1:T(8,128)S(1)} %fusion.2), channel_id=1, source_target_pairs={{0,2},{2,4},{4,6},{6,8},{8,10},{10,12},{12,14},{1,3},{3,5},{5,7},{... | collective-permute-start | bytes 1572872 | tf_op jit(solution)/shard_map/ppermute | solution.py:19
  362.0 9.3 collective-permute-done.32
  382.8 18.1 %collective-permute-done = f32[2,1,128]{2,0,1:T(2,128)S(1)} collective-permute-done((f32[2,1,128]{2,0,1:T(2,128)S(1)}, f32[2,1,128]{2,0,1:T(2,128)S(1)}, u32[]{:S(2)}, u32[]{:S(2)}) %collective-permute-start) | collective-permute-done | bytes 1056 | tf_op jit(solution)/shard_map/ppermute | solution.py:19
  400.9 44.2 %collective-permute-done.1 = f32[2,1,128]{2,0,1:T(2,128)S(1)} collective-permute-done((f32[2,1,128]{2,0,1:T(2,128)S(1)}, f32[2,1,128]{2,0,1:T(2,128)S(1)}, u32[]{:S(2)}, u32[]{:S(2)}) %collective-permute-start.1) | collective-permute-done | bytes 1056 | tf_op jit(solution)/shard_map/ppermute | solution.py:21
  445.1 11.7 collective-permute-start.3
  461.7 8.2 collective-permute-done.2
  475.3 13.3 %collective-permute-start.39 = (f32[1,3,128,512]{3,2,0,1:T(8,128)}, f32[1,3,128,512]{3,2,0,1:T(8,128)}, u32[]{:S(2)}, u32[]{:S(2)}) collective-permute-start(f32[1,3,128,512]{3,2,0,1:T(8,128)} %get-tuple-element.44), channel_id=1, source_target_pairs={{0,1},{2,3},{4,5},{6,7},{8,9},{10,11},{12,13},{14,15},{16,17},{18,... | collective-permute-start | bytes 2359304 | tf_op jit(solution)/shard_map/ppermute | solution.py:19
  490.0 13.6 %collective-permute-start.7 = (f32[1,3,128]{2,0,1:T(1,128)S(1)}, f32[1,3,128]{2,0,1:T(1,128)S(1)}, u32[]{:S(2)}, u32[]{:S(2)}) collective-permute-start(f32[1,3,128]{2,0,1:T(1,128)S(1)} %get-tuple-element.78), channel_id=1, source_target_pairs={{0,1},{2,3},{4,5},{6,7},{8,9},{10,11},{12,13},{14,15},{16,17},{18,... | collective-permute-start | bytes 4616 | tf_op jit(solution)/shard_map/ppermute | solution.py:19
  506.1 12.2 all-to-all-start
  518.4 7.7 collective-permute-done.6
  531.0 12.1 collective-permute-start.8
  550.0 39.2 %collective-permute-start.11 = (f32[1,3,128]{2,0,1:T(1,128)S(1)}, f32[1,3,128]{2,0,1:T(1,128)S(1)}, u32[]{:S(2)}, u32[]{:S(2)}) collective-permute-start(f32[1,3,128]{2,0,1:T(1,128)S(1)} %get-tuple-element.76), channel_id=1, source_target_pairs={{0,1},{2,3},{4,5},{6,7},{8,9},{10,11},{12,13},{14,15},{16,17},{18,... | collective-permute-start | bytes 4616 | tf_op jit(solution)/shard_map/ppermute | solution.py:19
  590.7 11.6 collective-permute-done.10
  613.0 120.6 %reduce-scatter.4.cloned.1.call-done = f32[32,512]{1,0:T(8,128)} async-done(((f32[512,512]{1,0:T(8,128)}), f32[32,512]{1,0:T(8,128)}) %reduce-scatter.4.cloned.1.call-update) | async-done | bytes 65552
  734.5 28.2 %collective-permute-start.40 = (f32[32,512]{0,1:T(8,128)S(1)}, f32[32,512]{0,1:T(8,128)S(1)}, u32[]{:S(2)}, u32[]{:S(2)}) collective-permute-start(f32[32,512]{0,1:T(8,128)S(1)} %copy.80), channel_id=1, source_target_pairs={{0,16},{16,0},{32,48},{48,32},{64,80},{80,64},{96,112},{112,96},{1... | collective-permute-start | bytes 196616 | tf_op jit(solution)/shard_map/ppermute | solution.py:35
  765.9 7.4 collective-permute-done.41
  785.4 10.5 collective-permute-done.18
  796.5 66.5 %all-reduce.3 = f32[512]{0:T(512)S(1)} all-reduce(f32[512]{0:T(512)S(1)} %bitcast.451), channel_id=3, replica_groups=mesh['scen'=32,'space'=8,'tm'=2] {'space','tm'}, use_global_device_ids=true, to_apply=%region_11.14.clone | all-reduce | flops 512 | bytes 4096
  863.1 11.6 collective-permute-start.42
  880.4 65.1 %all-reduce.2 = f32[512]{0:T(512)S(1)} all-reduce(f32[512]{0:T(512)S(1)} %subtract_dynamic-update-slice_fusion), channel_id=1, replica_groups=mesh['scen'=32,'space'=8,'tm'=2] {'space','tm'}, use_global_device_ids=true, to_apply=%add.2 | all-reduce | flops 512 | bytes 4096
  949.2 11.7 custom-call.55
  961.1 9.8 custom-call.56
  973.8 11.7 custom-call.57
  985.5 10.0 custom-call.58
  997.1 11.7 custom-call.59
  1008.8 9.8 custom-call.60
  1020.1 11.9 custom-call.61
  1036.6 10.4 while.2
  1047.0 40.1 %custom-call.51 = f32[4,128,128]{1,2,0:T(8,128)S(1)} custom-call(f32[4,128,128]{2,1,0:T(8,128)} %get-tuple-element.12), custom_call_target="InvertDiagBlocksLowerTriangular" | custom-call | tf_op jit(solution)/shard_map/triangular_solve | solution.py:41
  1096.7 75.3 %psum.15 = f32[256]{0:T(256)S(1)} all-reduce(f32[256]{0:T(256)S(1)} %broadcast_multiply_fusion), channel_id=1, replica_groups=mesh['scen'=32,'space'=8,'tm'=2] {'scen'}, use_global_device_ids=true, to_apply=%region_17.20 | all-reduce | flops 256 | bytes 2048 | tf_op jit(solution)/shard_map/psum | solution.py:118
  1172.1 72.5 %all-reduce.6.cloned.1.call-done = f32[256,256]{0,1:T(8,128)} async-done(((f32[256,256]{0,1:T(8,128)}), f32[256,256]{0,1:T(8,128)}) %all-reduce.6.cloned.1.call-update) | async-done | bytes 262160 | tf_op jit(solution)/shard_map/psum | solution.py:118
  1245.8 11.7 cholesky.104
  1257.6 9.8 custom-call.62
  1267.9 11.7 cholesky.114
  1287.5 20.8 %custom-call.52 = f32[2,128,128]{1,2,0:T(8,128)S(1)} custom-call(f32[2,128,128]{2,1,0:T(8,128)} %get-tuple-element.20), custom_call_target="InvertDiagBlocksLowerTriangular" | custom-call | tf_op jit(solution)/shard_map/triangular_solve | solution.py:41
  (283 shorter events, 160.4 us)
Async XLA Ops:
  53.4 12.1 collective-permute-start.20
  57.8 11.9 collective-permute-start.21
  70.1 36.3 %collective-permute-start.23 = (f32[1,3,128,512]{3,2,0,1:T(8,128)S(1)}, f32[1,3,128,512]{3,2,0,1:T(8,128)S(1)}, u32[]{:S(2)}, u32[]{:S(2)}) collective-permute-start(f32[1,3,128,512]{3,2,0,1:T(8,128)S(1)} %get-tuple-element.52), channel_id=1, source_target_pairs={{0,1},{2,3},{4,5},{6,7},{8,9},{10,11},{12,13},{14,15},{16,17},{18,... | collective-permute-start | bytes 2359304 | tf_op jit(solution)/shard_map/ppermute | solution.py:19
  87.2 36.7 %collective-permute-start.22 = (f32[1,3,128,512]{3,2,0,1:T(8,128)S(1)}, f32[1,3,128,512]{3,2,0,1:T(8,128)S(1)}, u32[]{:S(2)}, u32[]{:S(2)}) collective-permute-start(f32[1,3,128,512]{3,2,0,1:T(8,128)S(1)} %get-tuple-element.51), channel_id=1, source_target_pairs={{1,0},{3,2},{5,4},{7,6},{9,8},{11,10},{13,12},{15,14},{17,16},{19,... | collective-permute-start | bytes 2359304 | tf_op jit(solution)/shard_map/ppermute | solution.py:21
  124.6 52.8 %collective-permute-start.24 = (f32[2,1,128,512]{3,2,0,1:T(8,128)S(1)}, f32[2,1,128,512]{3,2,0,1:T(8,128)S(1)}, u32[]{:S(2)}, u32[]{:S(2)}) collective-permute-start(f32[2,1,128,512]{3,2,0,1:T(8,128)S(1)} %fusion.4), channel_id=1, source_target_pairs={{0,2},{2,4},{4,6},{6,8},{8,10},{10,12},{12,14},{1,3},{3,5},{5,7},{... | collective-permute-start | bytes 1572872 | tf_op jit(solution)/shard_map/ppermute | solution.py:19
  168.0 13.3 %collective-permute-start.25 = (f32[2,1,128,512]{3,2,0,1:T(8,128)S(1)}, f32[2,1,128,512]{3,2,0,1:T(8,128)S(1)}, u32[]{:S(2)}, u32[]{:S(2)}) collective-permute-start(f32[2,1,128,512]{3,2,0,1:T(8,128)S(1)} %fusion.4), channel_id=1, source_target_pairs={{2,0},{4,2},{6,4},{8,6},{10,8},{12,10},{14,12},{3,1},{5,3},{7,5},{... | collective-permute-start | bytes 1572872 | tf_op jit(solution)/shard_map/ppermute | solution.py:21
  181.7 10.7 collective-permute-start.27
  183.5 70.8 %collective-permute-start.26 = (f32[1,3,128,512]{3,2,0,1:T(8,128)S(1)}, f32[1,3,128,512]{3,2,0,1:T(8,128)S(1)}, u32[]{:S(2)}, u32[]{:S(2)}) collective-permute-start(f32[1,3,128,512]{3,2,0,1:T(8,128)S(1)} %get-tuple-element.49), channel_id=1, source_target_pairs={{1,0},{3,2},{5,4},{7,6},{9,8},{11,10},{13,12},{15,14},{17,16},{19,... | collective-permute-start | bytes 2359304 | tf_op jit(solution)/shard_map/ppermute | solution.py:21
  255.0 18.1 %collective-permute-start.28 = (f32[2,1,128,512]{3,2,0,1:T(8,128)S(1)}, f32[2,1,128,512]{3,2,0,1:T(8,128)S(1)}, u32[]{:S(2)}, u32[]{:S(2)}) collective-permute-start(f32[2,1,128,512]{3,2,0,1:T(8,128)S(1)} %fusion.3), channel_id=1, source_target_pairs={{0,2},{2,4},{4,6},{6,8},{8,10},{10,12},{12,14},{1,3},{3,5},{5,7},{... | collective-permute-start | bytes 1572872 | tf_op jit(solution)/shard_map/ppermute | solution.py:19
  263.1 13.9 %collective-permute-start.29 = (f32[2,1,128,512]{3,2,0,1:T(8,128)S(1)}, f32[2,1,128,512]{3,2,0,1:T(8,128)S(1)}, u32[]{:S(2)}, u32[]{:S(2)}) collective-permute-start(f32[2,1,128,512]{3,2,0,1:T(8,128)S(1)} %fusion.3), channel_id=1, source_target_pairs={{2,0},{4,2},{6,4},{8,6},{10,8},{12,10},{14,12},{3,1},{5,3},{7,5},{... | collective-permute-start | bytes 1572872 | tf_op jit(solution)/shard_map/ppermute | solution.py:21
  277.5 15.1 %collective-permute-start.31 = (f32[1,3,128,512]{3,2,0,1:T(8,128)S(1)}, f32[1,3,128,512]{3,2,0,1:T(8,128)S(1)}, u32[]{:S(2)}, u32[]{:S(2)}) collective-permute-start(f32[1,3,128,512]{3,2,0,1:T(8,128)S(1)} %get-tuple-element.48), channel_id=1, source_target_pairs={{0,1},{2,3},{4,5},{6,7},{8,9},{10,11},{12,13},{14,15},{16,17},{18,... | collective-permute-start | bytes 2359304 | tf_op jit(solution)/shard_map/ppermute | solution.py:19
  278.8 27.8 %collective-permute-start.30 = (f32[1,3,128,512]{3,2,0,1:T(8,128)S(1)}, f32[1,3,128,512]{3,2,0,1:T(8,128)S(1)}, u32[]{:S(2)}, u32[]{:S(2)}) collective-permute-start(f32[1,3,128,512]{3,2,0,1:T(8,128)S(1)} %get-tuple-element.47), channel_id=1, source_target_pairs={{1,0},{3,2},{5,4},{7,6},{9,8},{11,10},{13,12},{15,14},{17,16},{19,... | collective-permute-start | bytes 2359304 | tf_op jit(solution)/shard_map/ppermute | solution.py:21
  307.3 63.9 %collective-permute-start.32 = (f32[2,1,128,512]{3,2,0,1:T(8,128)S(1)}, f32[2,1,128,512]{3,2,0,1:T(8,128)S(1)}, u32[]{:S(2)}, u32[]{:S(2)}) collective-permute-start(f32[2,1,128,512]{3,2,0,1:T(8,128)S(1)} %fusion.2), channel_id=1, source_target_pairs={{0,2},{2,4},{4,6},{6,8},{8,10},{10,12},{12,14},{1,3},{3,5},{5,7},{... | collective-permute-start | bytes 1572872 | tf_op jit(solution)/shard_map/ppermute | solution.py:19
  360.7 14.4 %collective-permute-start.33 = (f32[2,1,128,512]{3,2,0,1:T(8,128)S(1)}, f32[2,1,128,512]{3,2,0,1:T(8,128)S(1)}, u32[]{:S(2)}, u32[]{:S(2)}) collective-permute-start(f32[2,1,128,512]{3,2,0,1:T(8,128)S(1)} %fusion.2), channel_id=1, source_target_pairs={{2,0},{4,2},{6,4},{8,6},{10,8},{12,10},{14,12},{3,1},{5,3},{7,5},{... | collective-permute-start | bytes 1572872 | tf_op jit(solution)/shard_map/ppermute | solution.py:21
  375.5 82.6 %collective-permute-start.35 = (f32[1,3,128,512]{3,2,0,1:T(8,128)S(1)}, f32[1,3,128,512]{3,2,0,1:T(8,128)S(1)}, u32[]{:S(2)}, u32[]{:S(2)}) collective-permute-start(f32[1,3,128,512]{3,2,0,1:T(8,128)S(1)} %get-tuple-element.46), channel_id=1, source_target_pairs={{0,1},{2,3},{4,5},{6,7},{8,9},{10,11},{12,13},{14,15},{16,17},{18,... | collective-permute-start | bytes 2359304 | tf_op jit(solution)/shard_map/ppermute | solution.py:19
  377.3 80.8 %collective-permute-start.34 = (f32[1,3,128,512]{3,2,0,1:T(8,128)S(1)}, f32[1,3,128,512]{3,2,0,1:T(8,128)S(1)}, u32[]{:S(2)}, u32[]{:S(2)}) collective-permute-start(f32[1,3,128,512]{3,2,0,1:T(8,128)S(1)} %get-tuple-element.45), channel_id=1, source_target_pairs={{1,0},{3,2},{5,4},{7,6},{9,8},{11,10},{13,12},{15,14},{17,16},{19,... | collective-permute-start | bytes 2359304 | tf_op jit(solution)/shard_map/ppermute | solution.py:21
  378.6 22.3 %collective-permute-start = (f32[2,1,128]{2,0,1:T(2,128)S(1)}, f32[2,1,128]{2,0,1:T(2,128)S(1)}, u32[]{:S(2)}, u32[]{:S(2)}) collective-permute-start(f32[2,1,128]{2,0,1:T(2,128)S(1)} %get-tuple-element.37), channel_id=1, source_target_pairs={{0,2},{2,4},{4,6},{6,8},{8,10},{10,12},{12,14},{1,3},{3,5},{5,7},{... | collective-permute-start | bytes 3080 | tf_op jit(solution)/shard_map/ppermute | solution.py:19
  380.8 64.3 %collective-permute-start.1 = (f32[2,1,128]{2,0,1:T(2,128)S(1)}, f32[2,1,128]{2,0,1:T(2,128)S(1)}, u32[]{:S(2)}, u32[]{:S(2)}) collective-permute-start(f32[2,1,128]{2,0,1:T(2,128)S(1)} %get-tuple-element.37), channel_id=1, source_target_pairs={{2,0},{4,2},{6,4},{8,6},{10,8},{12,10},{14,12},{3,1},{5,3},{7,5},{... | collective-permute-start | bytes 3080 | tf_op jit(solution)/shard_map/ppermute | solution.py:21
  445.1 16.6 %collective-permute-start.3 = (f32[1,3,128]{2,0,1:T(1,128)S(1)}, f32[1,3,128]{2,0,1:T(1,128)S(1)}, u32[]{:S(2)}, u32[]{:S(2)}) collective-permute-start(f32[1,3,128]{2,0,1:T(1,128)S(1)} %get-tuple-element.80), channel_id=1, source_target_pairs={{0,1},{2,3},{4,5},{6,7},{8,9},{10,11},{12,13},{14,15},{16,17},{18,... | collective-permute-start | bytes 4616 | tf_op jit(solution)/shard_map/ppermute | solution.py:19
  456.8 13.0 collective-permute-start.2
  458.9 14.3 %collective-permute-start.36 = (f32[2,1,128,512]{3,2,0,1:T(8,128)S(1)}, f32[2,1,128,512]{3,2,0,1:T(8,128)S(1)}, u32[]{:S(2)}, u32[]{:S(2)}) collective-permute-start(f32[2,1,128,512]{3,2,0,1:T(8,128)S(1)} %fusion.1), channel_id=1, source_target_pairs={{0,2},{2,4},{4,6},{6,8},{8,10},{10,12},{12,14},{1,3},{3,5},{5,7},{... | collective-permute-start | bytes 1572872 | tf_op jit(solution)/shard_map/ppermute | solution.py:19
  460.4 13.5 %collective-permute-start.37 = (f32[2,1,128,512]{3,2,0,1:T(8,128)S(1)}, f32[2,1,128,512]{3,2,0,1:T(8,128)S(1)}, u32[]{:S(2)}, u32[]{:S(2)}) collective-permute-start(f32[2,1,128,512]{3,2,0,1:T(8,128)S(1)} %fusion.1), channel_id=1, source_target_pairs={{2,0},{4,2},{6,4},{8,6},{10,8},{12,10},{14,12},{3,1},{5,3},{7,5},{... | collective-permute-start | bytes 1572872 | tf_op jit(solution)/shard_map/ppermute | solution.py:21
  470.3 19.7 %collective-permute-start.4 = (f32[2,1,128]{2,0,1:T(2,128)S(1)}, f32[2,1,128]{2,0,1:T(2,128)S(1)}, u32[]{:S(2)}, u32[]{:S(2)}) collective-permute-start(f32[2,1,128]{2,0,1:T(2,128)S(1)} %multiply_bitcast_fusion.3), channel_id=1, source_target_pairs={{0,2},{2,4},{4,6},{6,8},{8,10},{10,12},{12,14},{1,3},{3,5},{5,7},{... | collective-permute-start | bytes 3080 | tf_op jit(solution)/shard_map/ppermute | solution.py:19
  471.9 18.1 %collective-permute-start.5 = (f32[2,1,128]{2,0,1:T(2,128)S(1)}, f32[2,1,128]{2,0,1:T(2,128)S(1)}, u32[]{:S(2)}, u32[]{:S(2)}) collective-permute-start(f32[2,1,128]{2,0,1:T(2,128)S(1)} %multiply_bitcast_fusion.3), channel_id=1, source_target_pairs={{2,0},{4,2},{6,4},{8,6},{10,8},{12,10},{14,12},{3,1},{5,3},{7,5},{... | collective-permute-start | bytes 3080 | tf_op jit(solution)/shard_map/ppermute | solution.py:21
  475.3 50.8 %collective-permute-start.39 = (f32[1,3,128,512]{3,2,0,1:T(8,128)}, f32[1,3,128,512]{3,2,0,1:T(8,128)}, u32[]{:S(2)}, u32[]{:S(2)}) collective-permute-start(f32[1,3,128,512]{3,2,0,1:T(8,128)} %get-tuple-element.44), channel_id=1, source_target_pairs={{0,1},{2,3},{4,5},{6,7},{8,9},{10,11},{12,13},{14,15},{16,17},{18,... | collective-permute-start | bytes 2359304 | tf_op jit(solution)/shard_map/ppermute | solution.py:19
  488.6 37.4 %collective-permute-start.38 = (f32[1,3,128,512]{3,2,0,1:T(8,128)}, f32[1,3,128,512]{3,2,0,1:T(8,128)}, u32[]{:S(2)}, u32[]{:S(2)}) collective-permute-start(f32[1,3,128,512]{3,2,0,1:T(8,128)} %get-tuple-element.43), channel_id=1, source_target_pairs={{1,0},{3,2},{5,4},{7,6},{9,8},{11,10},{13,12},{15,14},{17,16},{19,... | collective-permute-start | bytes 2359304 | tf_op jit(solution)/shard_map/ppermute | solution.py:21
  490.0 28.4 %collective-permute-start.7 = (f32[1,3,128]{2,0,1:T(1,128)S(1)}, f32[1,3,128]{2,0,1:T(1,128)S(1)}, u32[]{:S(2)}, u32[]{:S(2)}) collective-permute-start(f32[1,3,128]{2,0,1:T(1,128)S(1)} %get-tuple-element.78), channel_id=1, source_target_pairs={{0,1},{2,3},{4,5},{6,7},{8,9},{10,11},{12,13},{14,15},{16,17},{18,... | collective-permute-start | bytes 4616 | tf_op jit(solution)/shard_map/ppermute | solution.py:19
  503.6 22.5 %collective-permute-start.6 = (f32[1,3,128]{2,0,1:T(1,128)S(1)}, f32[1,3,128]{2,0,1:T(1,128)S(1)}, u32[]{:S(2)}, u32[]{:S(2)}) collective-permute-start(f32[1,3,128]{2,0,1:T(1,128)S(1)} %get-tuple-element.77), channel_id=1, source_target_pairs={{1,0},{3,2},{5,4},{7,6},{9,8},{11,10},{13,12},{15,14},{17,16},{19,... | collective-permute-start | bytes 4616 | tf_op jit(solution)/shard_map/ppermute | solution.py:21
  506.1 439.4 %all-to-all-start = ((f32[16,32,256]{2,1,0:T(8,128)}), f32[16,32,256]{2,1,0:T(8,128)S(1)}, u32[]{:S(2)}, u32[]{:S(2)}) async-start(f32[16,32,256]{2,1,0:T(8,128)} %stack.2), calls=%async_computation | async-start | bytes 1048576 | tf_op jit(solution)/shard_map/all_to_all | solution.py:109
  518.3 215.2 %reduce-scatter.4.cloned.1.call-start = ((), (), s32[]{:S(2)}) async-start(), calls=%async_computation.4 | async-start | bytes 1114112
  530.7 415.6 %all-gather.2.cloned.1.call-start = ((), (), s32[]{:S(2)}) async-start(), calls=%async_computation.2 | async-start | bytes 1114112 | tf_op jit(solution)/shard_map/all_gather | solution.py:106
  531.0 14.1 %collective-permute-start.8 = (f32[2,1,128]{2,0,1:T(2,128)S(1)}, f32[2,1,128]{2,0,1:T(2,128)S(1)}, u32[]{:S(2)}, u32[]{:S(2)}) collective-permute-start(f32[2,1,128]{2,0,1:T(2,128)S(1)} %multiply_bitcast_fusion.2), channel_id=1, source_target_pairs={{0,2},{2,4},{4,6},{6,8},{8,10},{10,12},{12,14},{1,3},{3,5},{5,7},{... | collective-permute-start | bytes 3080 | tf_op jit(solution)/shard_map/ppermute | solution.py:19
  543.2 6.8 collective-permute-start.9
  550.0 40.7 %collective-permute-start.11 = (f32[1,3,128]{2,0,1:T(1,128)S(1)}, f32[1,3,128]{2,0,1:T(1,128)S(1)}, u32[]{:S(2)}, u32[]{:S(2)}) collective-permute-start(f32[1,3,128]{2,0,1:T(1,128)S(1)} %get-tuple-element.76), channel_id=1, source_target_pairs={{0,1},{2,3},{4,5},{6,7},{8,9},{10,11},{12,13},{14,15},{16,17},{18,... | collective-permute-start | bytes 4616 | tf_op jit(solution)/shard_map/ppermute | solution.py:19
  589.2 13.0 collective-permute-start.10
  602.6 3.4 collective-permute-start.12
  604.7 5.6 collective-permute-start.13
  610.4 155.4 %collective-permute-start.15 = (f32[1,3,128]{2,0,1:T(1,128)S(1)}, f32[1,3,128]{2,0,1:T(1,128)S(1)}, u32[]{:S(2)}, u32[]{:S(2)}) collective-permute-start(f32[1,3,128]{2,0,1:T(1,128)S(1)} %get-tuple-element.74), channel_id=1, source_target_pairs={{0,1},{2,3},{4,5},{6,7},{8,9},{10,11},{12,13},{14,15},{16,17},{18,... | collective-permute-start | bytes 4616 | tf_op jit(solution)/shard_map/ppermute | solution.py:19
  611.7 154.1 %collective-permute-start.14 = (f32[1,3,128]{2,0,1:T(1,128)S(1)}, f32[1,3,128]{2,0,1:T(1,128)S(1)}, u32[]{:S(2)}, u32[]{:S(2)}) collective-permute-start(f32[1,3,128]{2,0,1:T(1,128)S(1)} %get-tuple-element.73), channel_id=1, source_target_pairs={{1,0},{3,2},{5,4},{7,6},{9,8},{11,10},{13,12},{15,14},{17,16},{19,... | collective-permute-start | bytes 4616 | tf_op jit(solution)/shard_map/ppermute | solution.py:21
  734.5 29.3 %collective-permute-start.40 = (f32[32,512]{0,1:T(8,128)S(1)}, f32[32,512]{0,1:T(8,128)S(1)}, u32[]{:S(2)}, u32[]{:S(2)}) collective-permute-start(f32[32,512]{0,1:T(8,128)S(1)} %copy.80), channel_id=1, source_target_pairs={{0,16},{16,0},{32,48},{48,32},{64,80},{80,64},{96,112},{112,96},{1... | collective-permute-start | bytes 196616 | tf_op jit(solution)/shard_map/ppermute | solution.py:35
  763.9 9.4 collective-permute-start.41
  774.0 470.6 %all-reduce.6.cloned.1.call-start = ((), (), s32[]{:S(2)}) async-start(), calls=%async_computation.3 | async-start | bytes 524288 | tf_op jit(solution)/shard_map/psum | solution.py:118
  774.4 3.2 collective-permute-start.16
  776.3 4.3 collective-permute-start.17
  780.6 4.7 collective-permute-start.19
  781.9 14.0 %collective-permute-start.18 = (f32[1,3,128]{2,0,1:T(1,128)S(1)}, f32[1,3,128]{2,0,1:T(1,128)S(1)}, u32[]{:S(2)}, u32[]{:S(2)}) collective-permute-start(f32[1,3,128]{2,0,1:T(1,128)S(1)} %get-tuple-element.71), channel_id=1, source_target_pairs={{1,0},{3,2},{5,4},{7,6},{9,8},{11,10},{13,12},{15,14},{17,16},{19,... | collective-permute-start | bytes 4616 | tf_op jit(solution)/shard_map/ppermute | solution.py:21
  863.1 12.4 collective-permute-start.42
  875.6 4.7 collective-permute-start.43
  (18 other events, 1399.9 us)
Sparse Core Ops, SparseCore 0:
  530.8 202.6 reduce-scatter.3
  774.2 158.4 all-gather.1
  1096.5 148.0 all-reduce.5
